TPU v7x, 32 devices: a whole 2x2x4 slice. The times are simulated.
32 devices in a mesh: dom: 32 (over z, y, x, core).
Axes of the slice: x: 2, y: 2, z: 4, core: 2. Of those that a mesh axis runs over, the one named last changes fastest.
Arguments:
- features: bfloat16 [64, 262144], P(None, 'dom'), may hold values from -6 to 6
- cheb_weight: bfloat16 [4, 64, 64], replicated, may hold values from -0.375 to 0.375
- lap_tiles: bfloat16 [2048, 3, 128, 128], P('dom'), may hold values from -0.25 to 0.25
- col_index: int32 [2048, 3], P('dom'), may hold values from 0 to 63
- cross_tiles: bfloat16 [32, 5, 2, 128, 128], P('dom'), may hold values from -0.25 to 0.25
- send_index: int32 [32, 5, 2], P('dom'), may hold values from 0 to 63
- row_index: int32 [32, 5, 2], P('dom'), may hold values from 0 to 63
- pair_on: int32 [32, 5], P('dom'), may hold values 0 or 1
- blk_live: int32 [32], P('dom'), may hold values from 1 to 64, 1536 in all
- cotangent: bfloat16 [64, 262144], P(None, 'dom'), may hold values from -6 to 6
Outputs:
- conv_out: bfloat16 [64, 262144], P(None, 'dom')
- grad_x: bfloat16 [64, 262144], P(None, 'dom')
- grad_w: float32 [4, 64, 64], replicated
Inputs may be any that keep to these rules, and one draw needn't show every extreme that they name: `blk_live`: the counts sum to 1536 and the largest is exactly 64.
All inputs are finite; a program needn't handle non-finite values. No bound on the sum of `pair_on` or of `blk_live` on one device may be relied on, other than what follows from the above.
Results may differ from a plain program's by a relative error of at most 0.0059.
Values may be sent and summed in bfloat16 or wider, within the bound.
No kernel may reach another device: no remote copies, remote signals or barrier semaphores. Data moves between devices by JAX's collectives and lax.ppermute only.
A program may use at most 128 MiB of HBM per device.

v0:
```python
import jax
import jax.numpy as jnp
from jax import lax
from jax.sharding import PartitionSpec as P


def from_partner(block, axis, bit):
    count = lax.axis_size(axis)
    route = []
    for low in range(count):
        high = low | 1 << bit
        if high != low and high < count:
            route += [(low, high), (high, low)]
    return lax.ppermute(block, axis, route)


def local(
    features,
    cheb_weight,
    lap_tiles,
    col_index,
    cross_tiles,
    send_index,
    row_index,
    pair_on,
    blk_live,
    cotangent,
):
    channels = features.shape[0]
    block_count = lap_tiles.shape[0]
    block_size = lap_tiles.shape[2]
    rounds = cross_tiles.shape[1]
    live_blocks = blk_live[0]
    mask_half = (jnp.arange(block_count) < live_blocks).astype(jnp.bfloat16)[None, :, None]
    mask_full = mask_half.astype(jnp.float32)
    send_rows = send_index[0] % live_blocks
    recv_rows = row_index[0] % live_blocks
    switch = pair_on[0].astype(jnp.float32)
    coupling = cross_tiles[0]

    def apply_forward(values):
        gathered = jnp.take(values, col_index, axis=1)
        summed = jnp.einsum(
            "inab,finb->fia", lap_tiles, gathered, preferred_element_type=jnp.float32
        )
        for level in range(rounds):
            outgoing = jnp.take(values, send_rows[level], axis=1)
            incoming = from_partner(outgoing, "dom", level)
            product = jnp.einsum(
                "hab,fhb->fha", coupling[level], incoming, preferred_element_type=jnp.float32
            )
            summed = summed.at[:, recv_rows[level]].add(switch[level] * product)
        return summed

    def local_adjoint(values):
        terms = jnp.einsum("inab,fia->finb", lap_tiles, values, preferred_element_type=jnp.float32)
        return (
            jnp.zeros((channels, block_count, block_size), jnp.float32).at[:, col_index].add(terms)
        )

    flagged = coupling * pair_on[0].astype(jnp.bfloat16)[:, None, None, None]
    copies = [from_partner(flagged[level], "dom", level) for level in range(rounds)]

    def apply_adjoint(values):
        summed = local_adjoint(values)
        for level in range(rounds):
            slices = jnp.take(values, recv_rows[level], axis=1)
            incoming = from_partner(slices, "dom", level)
            contrib = jnp.einsum(
                "hab,fha->fhb", copies[level], incoming, preferred_element_type=jnp.float32
            )
            summed = summed.at[:, send_rows[level]].add(contrib)
        return summed

    zeroth = features.reshape(channels, block_count, block_size) * mask_half
    first = (apply_forward(zeroth) * mask_full).astype(jnp.bfloat16)
    second = ((2.0 * apply_forward(first) - zeroth.astype(jnp.float32)) * mask_full).astype(
        jnp.bfloat16
    )
    third = ((2.0 * apply_forward(second) - first.astype(jnp.float32)) * mask_full).astype(
        jnp.bfloat16
    )
    orders = jnp.stack([zeroth, first, second, third])
    output = (
        jnp.einsum("kfg,kfib->gib", cheb_weight, orders, preferred_element_type=jnp.float32)
        * mask_full
    )
    conv_out = output.astype(jnp.bfloat16).reshape(channels, block_count * block_size)
    upstream = cotangent.reshape(channels, block_count, block_size) * mask_half
    weight_terms = jnp.einsum("kfib,gib->kfg", orders, upstream, preferred_element_type=jnp.float32)
    grad_w = lax.psum(weight_terms, "dom")
    lifted = jnp.einsum("kfg,gib->kfib", cheb_weight, upstream, preferred_element_type=jnp.float32)
    back_third = (lifted[3] * mask_full).astype(jnp.bfloat16)
    adjoint_two = lifted[2] + 2.0 * apply_adjoint(back_third)
    back_second = (adjoint_two * mask_full).astype(jnp.bfloat16)
    adjoint_one = lifted[1] + 2.0 * apply_adjoint(back_second) - back_third.astype(jnp.float32)
    back_first = (adjoint_one * mask_full).astype(jnp.bfloat16)
    adjoint_zero = lifted[0] + apply_adjoint(back_first) - back_second.astype(jnp.float32)
    grad_x = (
        (adjoint_zero * mask_full).astype(jnp.bfloat16).reshape(channels, block_count * block_size)
    )
    return (conv_out, grad_x, grad_w)


def solution(mesh):
    in_specs = (
        P(None, "dom"),
        P(),
        P("dom", None, None, None),
        P("dom", None),
        P("dom", None, None, None, None),
        P("dom", None, None),
        P("dom", None, None),
        P("dom", None),
        P("dom"),
        P(None, "dom"),
    )
    out_specs = (P(None, "dom"), P(None, "dom"), P())
    return jax.shard_map(local, mesh=mesh, in_specs=in_specs, out_specs=out_specs, check_vma=False)
```

profile of v0, /device:TPU:0, one launch (start us, length us, event | category | flops | bytes accessed | tf_op | source)
XLA Modules:
  0.0 540.3 jit_solution(13784177287233342524)
XLA Ops:
  12.2 3.2 copy-done.3
  20.1 3.0 collective-permute-start.17
  57.3 3.2 slice_bitcast_fusion.3
  62.1 6.7 %fusion.42 = f32[64,64,3,128]{3,1,2,0:T(8,128)} fusion(bf16[64,3,128,128]{3,2,1,0:T(8,128)(2,1)} %param.16, bf16[64,64,128]{2,0,1:T(8,128)(2,1)S(1)} %fusion.13), kind=kOutput, calls=%fused_computation.133 | convolution fusion | flops 402653184 | bytes 13631488 | tf_op jit(solution)/shard_map/inab,fia->finb/dot_general | solution.py:56
  73.0 2.7 gather_fusion
  86.8 2.6 copy_multiply_fusion
  91.5 7.0 %fusion.22 = f32[64,64,128]{2,0,1:T(8,128)} fusion(bf16[64,3,128,128]{3,2,1,0:T(8,128)(2,1)} %param.16, bf16[64,3,64,128]{3,2,1,0:T(8,128)(2,1)S(1)} %bitcast.374, pred[64,3]{1,0:T(8,128)(4,1)S(1)} %copy.20), kind=kOutput, calls=%fused_computation.99 | convolution fusion | flops 404226048 | bytes 11534528 | tf_op jit(solution)/shard_map/inab,finb->fia/dot_general | solution.py:43
  102.2 20.1 %scatter_fusion.15 = f32[64,64,128]{2,0,1:T(8,128)S(1)} fusion(f32[64,64,128]{2,0,1:T(8,128)S(1)} %broadcast.220.clone, s32[192]{0:T(256)S(1)} %reshape.935, f32[192,64,128]{2,1,0:T(8,128)} %bitcast.367), kind=kCustom, calls=%fused_computation.48 | custom fusion | flops 1572864 | bytes 18875136 | tf_op jit(solution)/shard_map/scatter-add | solution.py:58
  134.9 2.9 collective-permute-start.4
  157.9 3.0 collective-permute-start.23
  177.8 6.7 %fusion.40 = f32[64,64,3,128]{3,1,2,0:T(8,128)} fusion(bf16[64,3,128,128]{3,2,1,0:T(8,128)(2,1)} %param.16, bf16[64,64,128]{2,0,1:T(8,128)(2,1)S(1)} %fusion.16), kind=kOutput, calls=%fused_computation.131 | convolution fusion | flops 402653184 | bytes 13631488 | tf_op jit(solution)/shard_map/inab,fia->finb/dot_general | solution.py:56
  202.4 2.9 collective-permute-start.29
  205.5 20.0 %scatter_fusion.21 = f32[64,64,128]{2,0,1:T(8,128)S(1)} fusion(f32[64,64,128]{2,0,1:T(8,128)S(1)} %broadcast.220, s32[192]{0:T(256)S(1)} %reshape.935, f32[192,64,128]{2,1,0:T(8,128)} %bitcast.368), kind=kCustom, calls=%fused_computation.54 | custom fusion | flops 1572864 | bytes 18875136 | tf_op jit(solution)/shard_map/scatter-add | solution.py:58
  243.8 2.2 scatter_fusion.26
  246.0 5.7 %fusion.20 = (bf16[64,64,128]{2,0,1:T(8,128)(2,1)S(1)}, bf16[64,64,128]{2,0,1:T(8,128)(2,1)}) fusion(f32[4,64,64,128]{3,1,2,0:T(8,128)} %copy-done.3, f32[64,64,128]{2,0,1:T(8,128)} %scatter_fusion.26, f32[64]{0:T(128)} %copy-done.32, f32[64,64,128]{2,0,1:T(8,128)} %scatter_fusion.4), kind=kLoop, calls=%fused_computation.91 | loop fusion | flops 5242880 | bytes 10486016 | tf_op jit(solution)/shard_map/convert_element_type | solution.py:97
  252.7 3.9 fusion.38
  266.2 4.0 gather_fusion.6
  270.1 2.5 gather_fusion.7
  272.6 2.5 gather_fusion.8
  275.1 2.5 gather_fusion.9
  277.6 2.5 gather_fusion.10
  280.1 2.5 gather_fusion.11
  287.3 8.1 %fusion.25 = f32[64,64,128]{2,0,1:T(8,128)} fusion(bf16[64,3,128,128]{3,2,1,0:T(8,128)(2,1)} %param.16, bf16[64,3,64,128]{3,2,1,0:T(8,128)(2,1)} %bitcast.373, pred[64,3]{1,0:T(8,128)(4,1)S(1)} %copy.20), kind=kOutput, calls=%fused_computation.100 | convolution fusion | flops 404226048 | bytes 11534528 | tf_op jit(solution)/shard_map/inab,finb->fia/dot_general | solution.py:43
  298.9 20.0 %scatter_fusion.27 = f32[64,64,128]{2,0,1:T(8,128)S(1)} fusion(f32[64,64,128]{2,0,1:T(8,128)S(1)} %copy-done.1, s32[192]{0:T(256)S(1)} %reshape.935, f32[192,64,128]{2,1,0:T(8,128)} %bitcast.366), kind=kCustom, calls=%fused_computation.60 | custom fusion | flops 1572864 | bytes 18875136 | tf_op jit(solution)/shard_map/scatter-add | solution.py:58
  329.6 2.9 collective-permute-start.9
  346.6 2.2 scatter_fusion.5
  359.0 4.2 fusion.36
  363.3 4.0 gather_fusion.12
  372.0 8.1 %fusion.28 = f32[64,64,128]{2,0,1:T(8,128)} fusion(bf16[64,3,128,128]{3,2,1,0:T(8,128)(2,1)} %param.16, bf16[64,3,64,128]{3,2,1,0:T(8,128)(2,1)} %bitcast.375, pred[64,3]{1,0:T(8,128)(4,1)S(1)} %copy.20), kind=kOutput, calls=%fused_computation.101 | convolution fusion | flops 404226048 | bytes 11534528 | tf_op jit(solution)/shard_map/inab,finb->fia/dot_general | solution.py:43
  394.7 2.2 scatter_fusion.13
  405.4 2.6 fusion.34
  409.2 122.6 %all-reduce.2.cloned.1.call-done = f32[4,64,64]{2,1,0:T(8,128)} async-done(((f32[4,64,64]{2,1,0:T(8,128)}), f32[4,64,64]{2,1,0:T(8,128)}) %all-reduce.2.cloned.1.call-update) | async-done | bytes 65552 | tf_op jit(solution)/shard_map/psum | solution.py:91
  (416 shorter events, 235.4 us)
Async XLA Ops:
  7.2 524.7 %all-reduce.2.cloned.1.call-start = ((), (), s32[]{:S(2)}) async-start(), calls=%async_computation | async-start | bytes 262144 | tf_op jit(solution)/shard_map/psum | solution.py:91
  17.0 137.2 %collective-permute-start.15 = (bf16[64,2,128]{2,0,1:T(8,128)(2,1)}, bf16[64,2,128]{2,0,1:T(8,128)(2,1)}, u32[]{:S(2)}, u32[]{:S(2)}) collective-permute-start(bf16[64,2,128]{2,0,1:T(8,128)(2,1)} %select_bitcast_fusion.14), channel_id=1, source_target_pairs={{0,1},{1,0},{2,3},{3,2},{4,5},{5,4},{6,7},{7,6},{8,9},{9,8},{10,11... | collective-permute-start | bytes 98312 | tf_op jit(solution)/shard_map/ppermute | solution.py:14
  18.8 135.5 %collective-permute-start.16 = (bf16[2,128,128]{2,1,0:T(8,128)(2,1)}, bf16[2,128,128]{2,1,0:T(8,128)(2,1)S(1)}, u32[]{:S(2)}, u32[]{:S(2)}) collective-permute-start(bf16[2,128,128]{2,1,0:T(8,128)(2,1)} %get-tuple-element.19), channel_id=1, source_target_pairs={{0,1},{1,0},{2,3},{3,2},{4,5},{5,4},{6,7},{7,6},{8,9},{9,8},{10,11... | collective-permute-start | bytes 196616 | tf_op jit(solution)/shard_map/ppermute | solution.py:14
  20.1 137.7 %collective-permute-start.17 = (bf16[64,2,128]{2,0,1:T(8,128)(2,1)}, bf16[64,2,128]{2,0,1:T(8,128)(2,1)}, u32[]{:S(2)}, u32[]{:S(2)}) collective-permute-start(bf16[64,2,128]{2,0,1:T(8,128)(2,1)} %select_bitcast_fusion.13), channel_id=1, source_target_pairs={{0,2},{2,0},{1,3},{3,1},{4,6},{6,4},{5,7},{7,5},{8,10},{10,8},{9,1... | collective-permute-start | bytes 98312 | tf_op jit(solution)/shard_map/ppermute | solution.py:14
  23.1 134.8 %collective-permute-start.18 = (bf16[2,128,128]{2,1,0:T(8,128)(2,1)}, bf16[2,128,128]{2,1,0:T(8,128)(2,1)}, u32[]{:S(2)}, u32[]{:S(2)}) collective-permute-start(bf16[2,128,128]{2,1,0:T(8,128)(2,1)} %get-tuple-element.18), channel_id=1, source_target_pairs={{0,2},{2,0},{1,3},{3,1},{4,6},{6,4},{5,7},{7,5},{8,10},{10,8},{9,1... | collective-permute-start | bytes 196616 | tf_op jit(solution)/shard_map/ppermute | solution.py:14
  28.6 93.7 %collective-permute-start = (bf16[64,2,128]{2,0,1:T(8,128)(2,1)}, bf16[64,2,128]{2,0,1:T(8,128)(2,1)}, u32[]{:S(2)}, u32[]{:S(2)}) collective-permute-start(bf16[64,2,128]{2,0,1:T(8,128)(2,1)} %select_bitcast_fusion.29), channel_id=1, source_target_pairs={{0,1},{1,0},{2,3},{3,2},{4,5},{5,4},{6,7},{7,6},{8,9},{9,8},{10,11... | collective-permute-start | bytes 98312 | tf_op jit(solution)/shard_map/ppermute | solution.py:14
  122.3 4.3 collective-permute-start.1
  134.9 5.0 collective-permute-start.4
  140.0 22.5 %collective-permute-start.19 = (bf16[64,2,128]{2,0,1:T(8,128)(2,1)}, bf16[64,2,128]{2,0,1:T(8,128)(2,1)}, u32[]{:S(2)}, u32[]{:S(2)}) collective-permute-start(bf16[64,2,128]{2,0,1:T(8,128)(2,1)} %select_bitcast_fusion.12), channel_id=1, source_target_pairs={{0,4},{4,0},{1,5},{5,1},{2,6},{6,2},{3,7},{7,3},{8,12},{12,8},{9,1... | collective-permute-start | bytes 98312 | tf_op jit(solution)/shard_map/ppermute | solution.py:14
  154.2 8.3 %collective-permute-start.20 = (bf16[2,128,128]{2,1,0:T(8,128)(2,1)}, bf16[2,128,128]{2,1,0:T(8,128)(2,1)S(1)}, u32[]{:S(2)}, u32[]{:S(2)}) collective-permute-start(bf16[2,128,128]{2,1,0:T(8,128)(2,1)} %get-tuple-element.17), channel_id=1, source_target_pairs={{0,4},{4,0},{1,5},{5,1},{2,6},{6,2},{3,7},{7,3},{8,12},{12,8},{9,1... | collective-permute-start | bytes 196616 | tf_op jit(solution)/shard_map/ppermute | solution.py:14
  154.3 9.7 %collective-permute-start.21 = (bf16[64,2,128]{2,0,1:T(8,128)(2,1)}, bf16[64,2,128]{2,0,1:T(8,128)(2,1)S(1)}, u32[]{:S(2)}, u32[]{:S(2)}) collective-permute-start(bf16[64,2,128]{2,0,1:T(8,128)(2,1)} %select_bitcast_fusion.11), channel_id=1, source_target_pairs={{0,8},{8,0},{1,9},{9,1},{2,10},{10,2},{3,11},{11,3},{4,12},{12,4},... | collective-permute-start | bytes 98312 | tf_op jit(solution)/shard_map/ppermute | solution.py:14
  157.8 6.2 %collective-permute-start.22 = (bf16[2,128,128]{2,1,0:T(8,128)(2,1)}, bf16[2,128,128]{2,1,0:T(8,128)(2,1)S(1)}, u32[]{:S(2)}, u32[]{:S(2)}) collective-permute-start(bf16[2,128,128]{2,1,0:T(8,128)(2,1)} %get-tuple-element.16), channel_id=1, source_target_pairs={{0,8},{8,0},{1,9},{9,1},{2,10},{10,2},{3,11},{11,3},{4,12},{12,4},... | collective-permute-start | bytes 196616 | tf_op jit(solution)/shard_map/ppermute | solution.py:14
  157.9 13.8 %collective-permute-start.23 = (bf16[64,2,128]{2,0,1:T(8,128)(2,1)}, bf16[64,2,128]{2,0,1:T(8,128)(2,1)}, u32[]{:S(2)}, u32[]{:S(2)}) collective-permute-start(bf16[64,2,128]{2,0,1:T(8,128)(2,1)} %select_bitcast_fusion.10), channel_id=1, source_target_pairs={{0,16},{16,0},{1,17},{17,1},{2,18},{18,2},{3,19},{19,3},{4,20},{20... | collective-permute-start | bytes 98312 | tf_op jit(solution)/shard_map/ppermute | solution.py:14
  162.5 9.2 %collective-permute-start.24 = (bf16[2,128,128]{2,1,0:T(8,128)(2,1)}, bf16[2,128,128]{2,1,0:T(8,128)(2,1)}, u32[]{:S(2)}, u32[]{:S(2)}) collective-permute-start(bf16[2,128,128]{2,1,0:T(8,128)(2,1)} %get-tuple-element.15), channel_id=1, source_target_pairs={{0,16},{16,0},{1,17},{17,1},{2,18},{18,2},{3,19},{19,3},{4,20},{20... | collective-permute-start | bytes 196616 | tf_op jit(solution)/shard_map/ppermute | solution.py:14
  194.7 32.1 %collective-permute-start.25 = (bf16[64,2,128]{2,0,1:T(8,128)(2,1)}, bf16[64,2,128]{2,0,1:T(8,128)(2,1)}, u32[]{:S(2)}, u32[]{:S(2)}) collective-permute-start(bf16[64,2,128]{2,0,1:T(8,128)(2,1)} %select_bitcast_fusion.9), channel_id=1, source_target_pairs={{0,1},{1,0},{2,3},{3,2},{4,5},{5,4},{6,7},{7,6},{8,9},{9,8},{10,11... | collective-permute-start | bytes 98312 | tf_op jit(solution)/shard_map/ppermute | solution.py:14
  195.4 33.1 %collective-permute-start.26 = (bf16[64,2,128]{2,0,1:T(8,128)(2,1)}, bf16[64,2,128]{2,0,1:T(8,128)(2,1)}, u32[]{:S(2)}, u32[]{:S(2)}) collective-permute-start(bf16[64,2,128]{2,0,1:T(8,128)(2,1)} %select_bitcast_fusion.8), channel_id=1, source_target_pairs={{0,2},{2,0},{1,3},{3,1},{4,6},{6,4},{5,7},{7,5},{8,10},{10,8},{9,1... | collective-permute-start | bytes 98312 | tf_op jit(solution)/shard_map/ppermute | solution.py:14
  197.9 32.2 %collective-permute-start.27 = (bf16[64,2,128]{2,0,1:T(8,128)(2,1)}, bf16[64,2,128]{2,0,1:T(8,128)(2,1)}, u32[]{:S(2)}, u32[]{:S(2)}) collective-permute-start(bf16[64,2,128]{2,0,1:T(8,128)(2,1)} %select_bitcast_fusion.7), channel_id=1, source_target_pairs={{0,4},{4,0},{1,5},{5,1},{2,6},{6,2},{3,7},{7,3},{8,12},{12,8},{9,1... | collective-permute-start | bytes 98312 | tf_op jit(solution)/shard_map/ppermute | solution.py:14
  200.1 31.7 %collective-permute-start.28 = (bf16[64,2,128]{2,0,1:T(8,128)(2,1)}, bf16[64,2,128]{2,0,1:T(8,128)(2,1)}, u32[]{:S(2)}, u32[]{:S(2)}) collective-permute-start(bf16[64,2,128]{2,0,1:T(8,128)(2,1)} %select_bitcast_fusion.6), channel_id=1, source_target_pairs={{0,8},{8,0},{1,9},{9,1},{2,10},{10,2},{3,11},{11,3},{4,12},{12,4},... | collective-permute-start | bytes 98312 | tf_op jit(solution)/shard_map/ppermute | solution.py:14
  202.4 39.8 %collective-permute-start.29 = (bf16[64,2,128]{2,0,1:T(8,128)(2,1)}, bf16[64,2,128]{2,0,1:T(8,128)(2,1)}, u32[]{:S(2)}, u32[]{:S(2)}) collective-permute-start(bf16[64,2,128]{2,0,1:T(8,128)(2,1)} %select_bitcast_fusion.5), channel_id=1, source_target_pairs={{0,16},{16,0},{1,17},{17,1},{2,18},{18,2},{3,19},{19,3},{4,20},{20... | collective-permute-start | bytes 98312 | tf_op jit(solution)/shard_map/ppermute | solution.py:14
  283.3 35.5 %collective-permute-start.30 = (bf16[64,2,128]{2,0,1:T(8,128)(2,1)}, bf16[64,2,128]{2,0,1:T(8,128)(2,1)}, u32[]{:S(2)}, u32[]{:S(2)}) collective-permute-start(bf16[64,2,128]{2,0,1:T(8,128)(2,1)} %select_bitcast_fusion.4), channel_id=1, source_target_pairs={{0,1},{1,0},{2,3},{3,2},{4,5},{5,4},{6,7},{7,6},{8,9},{9,8},{10,11... | collective-permute-start | bytes 98312 | tf_op jit(solution)/shard_map/ppermute | solution.py:14
  284.0 36.4 %collective-permute-start.31 = (bf16[64,2,128]{2,0,1:T(8,128)(2,1)}, bf16[64,2,128]{2,0,1:T(8,128)(2,1)}, u32[]{:S(2)}, u32[]{:S(2)}) collective-permute-start(bf16[64,2,128]{2,0,1:T(8,128)(2,1)} %select_bitcast_fusion.3), channel_id=1, source_target_pairs={{0,2},{2,0},{1,3},{3,1},{4,6},{6,4},{5,7},{7,5},{8,10},{10,8},{9,1... | collective-permute-start | bytes 98312 | tf_op jit(solution)/shard_map/ppermute | solution.py:14
  285.1 38.1 %collective-permute-start.32 = (bf16[64,2,128]{2,0,1:T(8,128)(2,1)}, bf16[64,2,128]{2,0,1:T(8,128)(2,1)}, u32[]{:S(2)}, u32[]{:S(2)}) collective-permute-start(bf16[64,2,128]{2,0,1:T(8,128)(2,1)} %select_bitcast_fusion.2), channel_id=1, source_target_pairs={{0,4},{4,0},{1,5},{5,1},{2,6},{6,2},{3,7},{7,3},{8,12},{12,8},{9,1... | collective-permute-start | bytes 98312 | tf_op jit(solution)/shard_map/ppermute | solution.py:14
  286.3 40.1 %collective-permute-start.33 = (bf16[64,2,128]{2,0,1:T(8,128)(2,1)}, bf16[64,2,128]{2,0,1:T(8,128)(2,1)}, u32[]{:S(2)}, u32[]{:S(2)}) collective-permute-start(bf16[64,2,128]{2,0,1:T(8,128)(2,1)} %select_bitcast_fusion.1), channel_id=1, source_target_pairs={{0,8},{8,0},{1,9},{9,1},{2,10},{10,2},{3,11},{11,3},{4,12},{12,4},... | collective-permute-start | bytes 98312 | tf_op jit(solution)/shard_map/ppermute | solution.py:14
  287.2 42.4 %collective-permute-start.34 = (bf16[64,2,128]{2,0,1:T(8,128)(2,1)}, bf16[64,2,128]{2,0,1:T(8,128)(2,1)}, u32[]{:S(2)}, u32[]{:S(2)}) collective-permute-start(bf16[64,2,128]{2,0,1:T(8,128)(2,1)} %select_bitcast_fusion), channel_id=1, source_target_pairs={{0,16},{16,0},{1,17},{17,1},{2,18},{18,2},{3,19},{19,3},{4,20},{20... | collective-permute-start | bytes 98312 | tf_op jit(solution)/shard_map/ppermute | solution.py:14
  318.8 15.3 %collective-permute-start.5 = (bf16[64,2,128]{2,0,1:T(8,128)(2,1)}, bf16[64,2,128]{2,0,1:T(8,128)(2,1)S(1)}, u32[]{:S(2)}, u32[]{:S(2)}) collective-permute-start(bf16[64,2,128]{2,0,1:T(8,128)(2,1)} %select_bitcast_fusion.24), channel_id=1, source_target_pairs={{0,1},{1,0},{2,3},{3,2},{4,5},{5,4},{6,7},{7,6},{8,9},{9,8},{10,11... | collective-permute-start | bytes 98312 | tf_op jit(solution)/shard_map/ppermute | solution.py:14
  320.4 15.1 %collective-permute-start.6 = (bf16[64,2,128]{2,0,1:T(8,128)(2,1)}, bf16[64,2,128]{2,0,1:T(8,128)(2,1)S(1)}, u32[]{:S(2)}, u32[]{:S(2)}) collective-permute-start(bf16[64,2,128]{2,0,1:T(8,128)(2,1)} %select_bitcast_fusion.23), channel_id=1, source_target_pairs={{0,2},{2,0},{1,3},{3,1},{4,6},{6,4},{5,7},{7,5},{8,10},{10,8},{9,1... | collective-permute-start | bytes 98312 | tf_op jit(solution)/shard_map/ppermute | solution.py:14
  323.3 13.7 %collective-permute-start.7 = (bf16[64,2,128]{2,0,1:T(8,128)(2,1)}, bf16[64,2,128]{2,0,1:T(8,128)(2,1)S(1)}, u32[]{:S(2)}, u32[]{:S(2)}) collective-permute-start(bf16[64,2,128]{2,0,1:T(8,128)(2,1)} %select_bitcast_fusion.22), channel_id=1, source_target_pairs={{0,4},{4,0},{1,5},{5,1},{2,6},{6,2},{3,7},{7,3},{8,12},{12,8},{9,1... | collective-permute-start | bytes 98312 | tf_op jit(solution)/shard_map/ppermute | solution.py:14
  326.4 11.9 %collective-permute-start.8 = (bf16[64,2,128]{2,0,1:T(8,128)(2,1)}, bf16[64,2,128]{2,0,1:T(8,128)(2,1)S(1)}, u32[]{:S(2)}, u32[]{:S(2)}) collective-permute-start(bf16[64,2,128]{2,0,1:T(8,128)(2,1)} %select_bitcast_fusion.21), channel_id=1, source_target_pairs={{0,8},{8,0},{1,9},{9,1},{2,10},{10,2},{3,11},{11,3},{4,12},{12,4},... | collective-permute-start | bytes 98312 | tf_op jit(solution)/shard_map/ppermute | solution.py:14
  329.6 25.8 %collective-permute-start.9 = (bf16[64,2,128]{2,0,1:T(8,128)(2,1)}, bf16[64,2,128]{2,0,1:T(8,128)(2,1)}, u32[]{:S(2)}, u32[]{:S(2)}) collective-permute-start(bf16[64,2,128]{2,0,1:T(8,128)(2,1)} %select_bitcast_fusion.20), channel_id=1, source_target_pairs={{0,16},{16,0},{1,17},{17,1},{2,18},{18,2},{3,19},{19,3},{4,20},{20... | collective-permute-start | bytes 98312 | tf_op jit(solution)/shard_map/ppermute | solution.py:14
  380.8 5.0 collective-permute-start.12
  381.4 5.8 %collective-permute-start.13 = (bf16[64,2,128]{2,0,1:T(8,128)(2,1)S(1)}, bf16[64,2,128]{2,0,1:T(8,128)(2,1)S(1)}, u32[]{:S(2)}, u32[]{:S(2)}) collective-permute-start(bf16[64,2,128]{2,0,1:T(8,128)(2,1)S(1)} %select_bitcast_fusion.16), channel_id=1, source_target_pairs={{0,8},{8,0},{1,9},{9,1},{2,10},{10,2},{3,11},{11,3},{4,12},{12,4},... | collective-permute-start | bytes 98312 | tf_op jit(solution)/shard_map/ppermute | solution.py:14
  382.4 14.5 %collective-permute-start.14 = (bf16[64,2,128]{2,0,1:T(8,128)(2,1)}, bf16[64,2,128]{2,0,1:T(8,128)(2,1)}, u32[]{:S(2)}, u32[]{:S(2)}) collective-permute-start(bf16[64,2,128]{2,0,1:T(8,128)(2,1)} %select_bitcast_fusion.15), channel_id=1, source_target_pairs={{0,16},{16,0},{1,17},{17,1},{2,18},{18,2},{3,19},{19,3},{4,20},{20... | collective-permute-start | bytes 98312 | tf_op jit(solution)/shard_map/ppermute | solution.py:14
  (89 other events, 799.8 us)
Sparse Core Ops, SparseCore 0:
  405.5 126.2 all-reduce.1
where the time goes:
time: 546 us; the launch traced here: 540 us
  other arithmetic  191 us (35%)
  waiting for transfers between devices  125 us (23%)
  matrix products  91 us (17%)
  local copies, waits for them, and re-layouts  80.2 us (15%)
  starting transfers between devices  37.6 us (7%)
  between operations  15.7 us (3%)
    psum x1, waiting for transfers between devices, local(): grad_w = lax.psum(weight_terms, 'dom')  123 us
    scatter-add x3, other arithmetic, local_adjoint(): jnp.zeros((channels, block_count, block_size), jnp.float32).at[:, col_index]  60 us
    ppermute x35, starting transfers between devices, from_partner(): return lax.ppermute(block, axis, route)  37.5 us
    scatter-add x15, other arithmetic, apply_forward(): summed = summed.at[:, recv_rows[level]].add(switch[level] * product)  32.2 us
    scatter-add x15, other arithmetic, apply_adjoint(): summed = summed.at[:, send_rows[level]].add(contrib)  25.6 us
    gather x15, local copies, waits for them, and re-layouts, apply_adjoint(): slices = jnp.take(values, recv_rows[level], axis=1)  23.7 us
    gather x15, local copies, waits for them, and re-layouts, apply_forward(): outgoing = jnp.take(values, send_rows[level], axis=1)  23.4 us
    dot_general x3, matrix products, apply_forward(): jnp.einsum('inab,finb->fia', lap_tiles, gathered, preferred_element_type=...  23.2 us
  transfers between devices with their start and end apart: 36, of which 5 were waited for; matrix products, arithmetic and copies ran while one was open for 46% of the time, Pallas kernels for 0%

commit v1 on v0

--- a/solution.py
+++ b/solution.py
@@ -88,7 +88,7 @@
     conv_out = output.astype(jnp.bfloat16).reshape(channels, block_count * block_size)
     upstream = cotangent.reshape(channels, block_count, block_size) * mask_half
     weight_terms = jnp.einsum("kfib,gib->kfg", orders, upstream, preferred_element_type=jnp.float32)
-    grad_w = lax.psum(weight_terms, "dom")
+    grad_w = jnp.sum(lax.all_gather(weight_terms, "dom"), axis=0)
     lifted = jnp.einsum("kfg,gib->kfib", cheb_weight, upstream, preferred_element_type=jnp.float32)
     back_third = (lifted[3] * mask_full).astype(jnp.bfloat16)
     adjoint_two = lifted[2] + 2.0 * apply_adjoint(back_third)

time: 546 us -> 485 us (0.89)
  waiting for transfers between devices: 125 us -> 61.5 us
    psum x1 -> x0, waiting for transfers between devices: 123 us -> none  [local(): grad_w = lax.psum(weight_terms, 'dom')]
    all_gather x0 -> x1, waiting for transfers between devices: none -> 57.7 us  [local(): grad_w = jnp.sum(lax.all_gather(weight_terms, 'dom'), axis=0)]
    unnamed x172 -> x171, local copies, waits for them, and re-layouts: 11.3 us -> 9.72 us
  transfers between devices with their start and end apart: 36 -> 36, of which waited for: 5 -> 6; matrix products, arithmetic and copies ran while one was open for 46% -> 52% of each run, Pallas kernels for 0% -> 0%
where the time goes in v1:
time: 485 us; the launch traced here: 479 us
  other arithmetic  194 us (40%)
  matrix products  89.5 us (18%)
  local copies, waits for them, and re-layouts  80.6 us (17%)
  waiting for transfers between devices  61.5 us (13%)
  starting transfers between devices  37.5 us (8%)
  between operations  15.8 us (3%)
    scatter-add x3, other arithmetic, local_adjoint(): jnp.zeros((channels, block_count, block_size), jnp.float32).at[:, col_index]  60 us
    all_gather x1, waiting for transfers between devices, local(): grad_w = jnp.sum(lax.all_gather(weight_terms, 'dom'), axis=0)  57.7 us
    ppermute x35, starting transfers between devices, from_partner(): return lax.ppermute(block, axis, route)  37.5 us
    scatter-add x15, other arithmetic, apply_forward(): summed = summed.at[:, recv_rows[level]].add(switch[level] * product)  32.4 us
    scatter-add x15, other arithmetic, apply_adjoint(): summed = summed.at[:, send_rows[level]].add(contrib)  25.6 us
    gather x15, local copies, waits for them, and re-layouts, apply_forward(): outgoing = jnp.take(values, send_rows[level], axis=1)  24 us
    gather x15, local copies, waits for them, and re-layouts, apply_adjoint(): slices = jnp.take(values, recv_rows[level], axis=1)  23.7 us
    dot_general x3, matrix products, apply_forward(): jnp.einsum('inab,finb->fia', lap_tiles, gathered, preferred_element_type=...  23.1 us
  transfers between devices with their start and end apart: 36, of which 6 were waited for; matrix products, arithmetic and copies ran while one was open for 52% of the time, Pallas kernels for 0%

profile of v1, /device:TPU:0, one launch (start us, length us, event | category | flops | bytes accessed | tf_op | source)
XLA Modules:
  0.0 478.8 jit_solution(9509345949319660239)
XLA Ops:
  12.2 3.2 copy-done.3
  20.1 3.0 collective-permute-start.17
  57.3 3.2 slice_bitcast_fusion.3
  62.1 6.7 %fusion.42 = f32[64,64,3,128]{3,1,2,0:T(8,128)} fusion(bf16[64,3,128,128]{3,2,1,0:T(8,128)(2,1)} %param.16, bf16[64,64,128]{2,0,1:T(8,128)(2,1)S(1)} %fusion.13), kind=kOutput, calls=%fused_computation.133 | convolution fusion | flops 402653184 | bytes 13631488 | tf_op jit(solution)/shard_map/inab,fia->finb/dot_general | solution.py:56
  73.0 2.7 gather_fusion
  86.8 2.6 copy_multiply_fusion
  91.5 7.0 %fusion.22 = f32[64,64,128]{2,0,1:T(8,128)} fusion(bf16[64,3,128,128]{3,2,1,0:T(8,128)(2,1)} %param.16, bf16[64,3,64,128]{3,2,1,0:T(8,128)(2,1)S(1)} %bitcast.375, pred[64,3]{1,0:T(8,128)(4,1)S(1)} %copy.35), kind=kOutput, calls=%fused_computation.99 | convolution fusion | flops 404226048 | bytes 11534528 | tf_op jit(solution)/shard_map/inab,finb->fia/dot_general | solution.py:43
  102.2 20.1 %scatter_fusion.15 = f32[64,64,128]{2,0,1:T(8,128)S(1)} fusion(f32[64,64,128]{2,0,1:T(8,128)S(1)} %broadcast.220.clone, s32[192]{0:T(256)S(1)} %reshape.936, f32[192,64,128]{2,1,0:T(8,128)} %bitcast.368), kind=kCustom, calls=%fused_computation.48 | custom fusion | flops 1572864 | bytes 18875136 | tf_op jit(solution)/shard_map/scatter-add | solution.py:58
  134.9 2.9 collective-permute-start.4
  157.9 3.0 collective-permute-start.23
  177.8 6.7 %fusion.40 = f32[64,64,3,128]{3,1,2,0:T(8,128)} fusion(bf16[64,3,128,128]{3,2,1,0:T(8,128)(2,1)} %param.16, bf16[64,64,128]{2,0,1:T(8,128)(2,1)S(1)} %fusion.16), kind=kOutput, calls=%fused_computation.131 | convolution fusion | flops 402653184 | bytes 13631488 | tf_op jit(solution)/shard_map/inab,fia->finb/dot_general | solution.py:56
  202.4 2.9 collective-permute-start.29
  205.5 20.0 %scatter_fusion.21 = f32[64,64,128]{2,0,1:T(8,128)S(1)} fusion(f32[64,64,128]{2,0,1:T(8,128)S(1)} %broadcast.220, s32[192]{0:T(256)S(1)} %reshape.936, f32[192,64,128]{2,1,0:T(8,128)} %bitcast.369), kind=kCustom, calls=%fused_computation.54 | custom fusion | flops 1572864 | bytes 18875136 | tf_op jit(solution)/shard_map/scatter-add | solution.py:58
  246.0 5.7 %fusion.20 = (bf16[64,64,128]{2,0,1:T(8,128)(2,1)S(1)}, bf16[64,64,128]{2,0,1:T(8,128)(2,1)}) fusion(f32[4,64,64,128]{3,1,2,0:T(8,128)} %copy-done.3, f32[64,64,128]{2,0,1:T(8,128)} %scatter_fusion.26, f32[64]{0:T(128)} %copy-done.34, f32[64,64,128]{2,0,1:T(8,128)} %scatter_fusion.4), kind=kLoop, calls=%fused_computation.91 | loop fusion | flops 5242880 | bytes 10486016 | tf_op jit(solution)/shard_map/convert_element_type | solution.py:97
  252.7 3.9 fusion.38
  266.2 4.0 gather_fusion.6
  270.1 2.5 gather_fusion.7
  272.6 2.5 gather_fusion.8
  275.1 2.5 gather_fusion.9
  277.6 2.5 gather_fusion.10
  280.1 2.5 gather_fusion.11
  287.3 8.1 %fusion.25 = f32[64,64,128]{2,0,1:T(8,128)} fusion(bf16[64,3,128,128]{3,2,1,0:T(8,128)(2,1)} %param.16, bf16[64,3,64,128]{3,2,1,0:T(8,128)(2,1)} %bitcast.374, pred[64,3]{1,0:T(8,128)(4,1)S(1)} %copy.35), kind=kOutput, calls=%fused_computation.100 | convolution fusion | flops 404226048 | bytes 11534528 | tf_op jit(solution)/shard_map/inab,finb->fia/dot_general | solution.py:43
  298.9 20.0 %scatter_fusion.27 = f32[64,64,128]{2,0,1:T(8,128)S(1)} fusion(f32[64,64,128]{2,0,1:T(8,128)S(1)} %copy-done.1, s32[192]{0:T(256)S(1)} %reshape.936, f32[192,64,128]{2,1,0:T(8,128)} %bitcast.367), kind=kCustom, calls=%fused_computation.60 | custom fusion | flops 1572864 | bytes 18875136 | tf_op jit(solution)/shard_map/scatter-add | solution.py:58
  329.6 2.9 collective-permute-start.9
  346.6 2.2 scatter_fusion.5
  359.0 4.2 fusion.36
  363.3 4.0 gather_fusion.12
  372.6 8.0 %fusion.28 = f32[64,64,128]{2,0,1:T(8,128)} fusion(bf16[64,3,128,128]{3,2,1,0:T(8,128)(2,1)} %param.16, bf16[64,3,64,128]{3,2,1,0:T(8,128)(2,1)} %bitcast.376, pred[64,3]{1,0:T(8,128)(4,1)S(1)} %copy.35), kind=kOutput, calls=%fused_computation.101 | convolution fusion | flops 404226048 | bytes 11534528 | tf_op jit(solution)/shard_map/inab,finb->fia/dot_general | solution.py:43
  390.9 2.2 scatter_fusion.11
  406.1 2.5 copy.74
  410.9 57.7 %all-gather.3.cloned.1.call-done = f32[128,64,64]{2,1,0:T(8,128)} async-done(((f32[4,64,64]{2,1,0:T(8,128)}), f32[128,64,64]{2,1,0:T(8,128)}) %all-gather.3.cloned.1.call-update) | async-done | bytes 2097168 | tf_op jit(solution)/shard_map/all_gather | solution.py:91
  468.7 3.3 reduce_sum.9
  (416 shorter events, 237.9 us)
Async XLA Ops:
  7.2 461.5 %all-gather.3.cloned.1.call-start = ((), (), s32[]{:S(2)}) async-start(), calls=%async_computation | async-start | bytes 4325376 | tf_op jit(solution)/shard_map/all_gather | solution.py:91
  17.0 137.2 %collective-permute-start.15 = (bf16[64,2,128]{2,0,1:T(8,128)(2,1)}, bf16[64,2,128]{2,0,1:T(8,128)(2,1)}, u32[]{:S(2)}, u32[]{:S(2)}) collective-permute-start(bf16[64,2,128]{2,0,1:T(8,128)(2,1)} %select_bitcast_fusion.14), channel_id=1, source_target_pairs={{0,1},{1,0},{2,3},{3,2},{4,5},{5,4},{6,7},{7,6},{8,9},{9,8},{10,11... | collective-permute-start | bytes 98312 | tf_op jit(solution)/shard_map/ppermute | solution.py:14
  18.8 135.5 %collective-permute-start.16 = (bf16[2,128,128]{2,1,0:T(8,128)(2,1)}, bf16[2,128,128]{2,1,0:T(8,128)(2,1)S(1)}, u32[]{:S(2)}, u32[]{:S(2)}) collective-permute-start(bf16[2,128,128]{2,1,0:T(8,128)(2,1)} %get-tuple-element.19), channel_id=1, source_target_pairs={{0,1},{1,0},{2,3},{3,2},{4,5},{5,4},{6,7},{7,6},{8,9},{9,8},{10,11... | collective-permute-start | bytes 196616 | tf_op jit(solution)/shard_map/ppermute | solution.py:14
  20.1 137.7 %collective-permute-start.17 = (bf16[64,2,128]{2,0,1:T(8,128)(2,1)}, bf16[64,2,128]{2,0,1:T(8,128)(2,1)}, u32[]{:S(2)}, u32[]{:S(2)}) collective-permute-start(bf16[64,2,128]{2,0,1:T(8,128)(2,1)} %select_bitcast_fusion.13), channel_id=1, source_target_pairs={{0,2},{2,0},{1,3},{3,1},{4,6},{6,4},{5,7},{7,5},{8,10},{10,8},{9,1... | collective-permute-start | bytes 98312 | tf_op jit(solution)/shard_map/ppermute | solution.py:14
  23.1 134.8 %collective-permute-start.18 = (bf16[2,128,128]{2,1,0:T(8,128)(2,1)}, bf16[2,128,128]{2,1,0:T(8,128)(2,1)}, u32[]{:S(2)}, u32[]{:S(2)}) collective-permute-start(bf16[2,128,128]{2,1,0:T(8,128)(2,1)} %get-tuple-element.18), channel_id=1, source_target_pairs={{0,2},{2,0},{1,3},{3,1},{4,6},{6,4},{5,7},{7,5},{8,10},{10,8},{9,1... | collective-permute-start | bytes 196616 | tf_op jit(solution)/shard_map/ppermute | solution.py:14
  28.6 93.7 %collective-permute-start = (bf16[64,2,128]{2,0,1:T(8,128)(2,1)}, bf16[64,2,128]{2,0,1:T(8,128)(2,1)}, u32[]{:S(2)}, u32[]{:S(2)}) collective-permute-start(bf16[64,2,128]{2,0,1:T(8,128)(2,1)} %select_bitcast_fusion.29), channel_id=1, source_target_pairs={{0,1},{1,0},{2,3},{3,2},{4,5},{5,4},{6,7},{7,6},{8,9},{9,8},{10,11... | collective-permute-start | bytes 98312 | tf_op jit(solution)/shard_map/ppermute | solution.py:14
  122.3 4.3 collective-permute-start.1
  134.9 5.0 %collective-permute-start.4 = (bf16[64,2,128]{2,0,1:T(8,128)(2,1)}, bf16[64,2,128]{2,0,1:T(8,128)(2,1)S(1)}, u32[]{:S(2)}, u32[]{:S(2)}) collective-permute-start(bf16[64,2,128]{2,0,1:T(8,128)(2,1)} %select_bitcast_fusion.25), channel_id=1, source_target_pairs={{0,16},{16,0},{1,17},{17,1},{2,18},{18,2},{3,19},{19,3},{4,20},{20... | collective-permute-start | bytes 98312 | tf_op jit(solution)/shard_map/ppermute | solution.py:14
  140.0 22.5 %collective-permute-start.19 = (bf16[64,2,128]{2,0,1:T(8,128)(2,1)}, bf16[64,2,128]{2,0,1:T(8,128)(2,1)}, u32[]{:S(2)}, u32[]{:S(2)}) collective-permute-start(bf16[64,2,128]{2,0,1:T(8,128)(2,1)} %select_bitcast_fusion.12), channel_id=1, source_target_pairs={{0,4},{4,0},{1,5},{5,1},{2,6},{6,2},{3,7},{7,3},{8,12},{12,8},{9,1... | collective-permute-start | bytes 98312 | tf_op jit(solution)/shard_map/ppermute | solution.py:14
  154.2 8.3 %collective-permute-start.20 = (bf16[2,128,128]{2,1,0:T(8,128)(2,1)}, bf16[2,128,128]{2,1,0:T(8,128)(2,1)S(1)}, u32[]{:S(2)}, u32[]{:S(2)}) collective-permute-start(bf16[2,128,128]{2,1,0:T(8,128)(2,1)} %get-tuple-element.17), channel_id=1, source_target_pairs={{0,4},{4,0},{1,5},{5,1},{2,6},{6,2},{3,7},{7,3},{8,12},{12,8},{9,1... | collective-permute-start | bytes 196616 | tf_op jit(solution)/shard_map/ppermute | solution.py:14
  154.3 9.7 %collective-permute-start.21 = (bf16[64,2,128]{2,0,1:T(8,128)(2,1)}, bf16[64,2,128]{2,0,1:T(8,128)(2,1)S(1)}, u32[]{:S(2)}, u32[]{:S(2)}) collective-permute-start(bf16[64,2,128]{2,0,1:T(8,128)(2,1)} %select_bitcast_fusion.11), channel_id=1, source_target_pairs={{0,8},{8,0},{1,9},{9,1},{2,10},{10,2},{3,11},{11,3},{4,12},{12,4},... | collective-permute-start | bytes 98312 | tf_op jit(solution)/shard_map/ppermute | solution.py:14
  157.8 6.2 %collective-permute-start.22 = (bf16[2,128,128]{2,1,0:T(8,128)(2,1)}, bf16[2,128,128]{2,1,0:T(8,128)(2,1)S(1)}, u32[]{:S(2)}, u32[]{:S(2)}) collective-permute-start(bf16[2,128,128]{2,1,0:T(8,128)(2,1)} %get-tuple-element.16), channel_id=1, source_target_pairs={{0,8},{8,0},{1,9},{9,1},{2,10},{10,2},{3,11},{11,3},{4,12},{12,4},... | collective-permute-start | bytes 196616 | tf_op jit(solution)/shard_map/ppermute | solution.py:14
  157.9 13.8 %collective-permute-start.23 = (bf16[64,2,128]{2,0,1:T(8,128)(2,1)}, bf16[64,2,128]{2,0,1:T(8,128)(2,1)}, u32[]{:S(2)}, u32[]{:S(2)}) collective-permute-start(bf16[64,2,128]{2,0,1:T(8,128)(2,1)} %select_bitcast_fusion.10), channel_id=1, source_target_pairs={{0,16},{16,0},{1,17},{17,1},{2,18},{18,2},{3,19},{19,3},{4,20},{20... | collective-permute-start | bytes 98312 | tf_op jit(solution)/shard_map/ppermute | solution.py:14
  162.5 9.2 %collective-permute-start.24 = (bf16[2,128,128]{2,1,0:T(8,128)(2,1)}, bf16[2,128,128]{2,1,0:T(8,128)(2,1)}, u32[]{:S(2)}, u32[]{:S(2)}) collective-permute-start(bf16[2,128,128]{2,1,0:T(8,128)(2,1)} %get-tuple-element.15), channel_id=1, source_target_pairs={{0,16},{16,0},{1,17},{17,1},{2,18},{18,2},{3,19},{19,3},{4,20},{20... | collective-permute-start | bytes 196616 | tf_op jit(solution)/shard_map/ppermute | solution.py:14
  194.7 32.1 %collective-permute-start.25 = (bf16[64,2,128]{2,0,1:T(8,128)(2,1)}, bf16[64,2,128]{2,0,1:T(8,128)(2,1)}, u32[]{:S(2)}, u32[]{:S(2)}) collective-permute-start(bf16[64,2,128]{2,0,1:T(8,128)(2,1)} %select_bitcast_fusion.9), channel_id=1, source_target_pairs={{0,1},{1,0},{2,3},{3,2},{4,5},{5,4},{6,7},{7,6},{8,9},{9,8},{10,11... | collective-permute-start | bytes 98312 | tf_op jit(solution)/shard_map/ppermute | solution.py:14
  195.4 33.1 %collective-permute-start.26 = (bf16[64,2,128]{2,0,1:T(8,128)(2,1)}, bf16[64,2,128]{2,0,1:T(8,128)(2,1)}, u32[]{:S(2)}, u32[]{:S(2)}) collective-permute-start(bf16[64,2,128]{2,0,1:T(8,128)(2,1)} %select_bitcast_fusion.8), channel_id=1, source_target_pairs={{0,2},{2,0},{1,3},{3,1},{4,6},{6,4},{5,7},{7,5},{8,10},{10,8},{9,1... | collective-permute-start | bytes 98312 | tf_op jit(solution)/shard_map/ppermute | solution.py:14
  197.9 32.2 %collective-permute-start.27 = (bf16[64,2,128]{2,0,1:T(8,128)(2,1)}, bf16[64,2,128]{2,0,1:T(8,128)(2,1)}, u32[]{:S(2)}, u32[]{:S(2)}) collective-permute-start(bf16[64,2,128]{2,0,1:T(8,128)(2,1)} %select_bitcast_fusion.7), channel_id=1, source_target_pairs={{0,4},{4,0},{1,5},{5,1},{2,6},{6,2},{3,7},{7,3},{8,12},{12,8},{9,1... | collective-permute-start | bytes 98312 | tf_op jit(solution)/shard_map/ppermute | solution.py:14
  200.1 31.7 %collective-permute-start.28 = (bf16[64,2,128]{2,0,1:T(8,128)(2,1)}, bf16[64,2,128]{2,0,1:T(8,128)(2,1)}, u32[]{:S(2)}, u32[]{:S(2)}) collective-permute-start(bf16[64,2,128]{2,0,1:T(8,128)(2,1)} %select_bitcast_fusion.6), channel_id=1, source_target_pairs={{0,8},{8,0},{1,9},{9,1},{2,10},{10,2},{3,11},{11,3},{4,12},{12,4},... | collective-permute-start | bytes 98312 | tf_op jit(solution)/shard_map/ppermute | solution.py:14
  202.4 39.8 %collective-permute-start.29 = (bf16[64,2,128]{2,0,1:T(8,128)(2,1)}, bf16[64,2,128]{2,0,1:T(8,128)(2,1)}, u32[]{:S(2)}, u32[]{:S(2)}) collective-permute-start(bf16[64,2,128]{2,0,1:T(8,128)(2,1)} %select_bitcast_fusion.5), channel_id=1, source_target_pairs={{0,16},{16,0},{1,17},{17,1},{2,18},{18,2},{3,19},{19,3},{4,20},{20... | collective-permute-start | bytes 98312 | tf_op jit(solution)/shard_map/ppermute | solution.py:14
  283.3 35.5 %collective-permute-start.30 = (bf16[64,2,128]{2,0,1:T(8,128)(2,1)}, bf16[64,2,128]{2,0,1:T(8,128)(2,1)}, u32[]{:S(2)}, u32[]{:S(2)}) collective-permute-start(bf16[64,2,128]{2,0,1:T(8,128)(2,1)} %select_bitcast_fusion.4), channel_id=1, source_target_pairs={{0,1},{1,0},{2,3},{3,2},{4,5},{5,4},{6,7},{7,6},{8,9},{9,8},{10,11... | collective-permute-start | bytes 98312 | tf_op jit(solution)/shard_map/ppermute | solution.py:14
  284.0 36.4 %collective-permute-start.31 = (bf16[64,2,128]{2,0,1:T(8,128)(2,1)}, bf16[64,2,128]{2,0,1:T(8,128)(2,1)}, u32[]{:S(2)}, u32[]{:S(2)}) collective-permute-start(bf16[64,2,128]{2,0,1:T(8,128)(2,1)} %select_bitcast_fusion.3), channel_id=1, source_target_pairs={{0,2},{2,0},{1,3},{3,1},{4,6},{6,4},{5,7},{7,5},{8,10},{10,8},{9,1... | collective-permute-start | bytes 98312 | tf_op jit(solution)/shard_map/ppermute | solution.py:14
  285.1 38.2 %collective-permute-start.32 = (bf16[64,2,128]{2,0,1:T(8,128)(2,1)}, bf16[64,2,128]{2,0,1:T(8,128)(2,1)}, u32[]{:S(2)}, u32[]{:S(2)}) collective-permute-start(bf16[64,2,128]{2,0,1:T(8,128)(2,1)} %select_bitcast_fusion.2), channel_id=1, source_target_pairs={{0,4},{4,0},{1,5},{5,1},{2,6},{6,2},{3,7},{7,3},{8,12},{12,8},{9,1... | collective-permute-start | bytes 98312 | tf_op jit(solution)/shard_map/ppermute | solution.py:14
  286.3 40.1 %collective-permute-start.33 = (bf16[64,2,128]{2,0,1:T(8,128)(2,1)}, bf16[64,2,128]{2,0,1:T(8,128)(2,1)}, u32[]{:S(2)}, u32[]{:S(2)}) collective-permute-start(bf16[64,2,128]{2,0,1:T(8,128)(2,1)} %select_bitcast_fusion.1), channel_id=1, source_target_pairs={{0,8},{8,0},{1,9},{9,1},{2,10},{10,2},{3,11},{11,3},{4,12},{12,4},... | collective-permute-start | bytes 98312 | tf_op jit(solution)/shard_map/ppermute | solution.py:14
  287.2 42.4 %collective-permute-start.34 = (bf16[64,2,128]{2,0,1:T(8,128)(2,1)}, bf16[64,2,128]{2,0,1:T(8,128)(2,1)}, u32[]{:S(2)}, u32[]{:S(2)}) collective-permute-start(bf16[64,2,128]{2,0,1:T(8,128)(2,1)} %select_bitcast_fusion), channel_id=1, source_target_pairs={{0,16},{16,0},{1,17},{17,1},{2,18},{18,2},{3,19},{19,3},{4,20},{20... | collective-permute-start | bytes 98312 | tf_op jit(solution)/shard_map/ppermute | solution.py:14
  318.8 15.3 %collective-permute-start.5 = (bf16[64,2,128]{2,0,1:T(8,128)(2,1)}, bf16[64,2,128]{2,0,1:T(8,128)(2,1)S(1)}, u32[]{:S(2)}, u32[]{:S(2)}) collective-permute-start(bf16[64,2,128]{2,0,1:T(8,128)(2,1)} %select_bitcast_fusion.24), channel_id=1, source_target_pairs={{0,1},{1,0},{2,3},{3,2},{4,5},{5,4},{6,7},{7,6},{8,9},{9,8},{10,11... | collective-permute-start | bytes 98312 | tf_op jit(solution)/shard_map/ppermute | solution.py:14
  320.4 15.1 %collective-permute-start.6 = (bf16[64,2,128]{2,0,1:T(8,128)(2,1)}, bf16[64,2,128]{2,0,1:T(8,128)(2,1)S(1)}, u32[]{:S(2)}, u32[]{:S(2)}) collective-permute-start(bf16[64,2,128]{2,0,1:T(8,128)(2,1)} %select_bitcast_fusion.23), channel_id=1, source_target_pairs={{0,2},{2,0},{1,3},{3,1},{4,6},{6,4},{5,7},{7,5},{8,10},{10,8},{9,1... | collective-permute-start | bytes 98312 | tf_op jit(solution)/shard_map/ppermute | solution.py:14
  323.3 13.7 %collective-permute-start.7 = (bf16[64,2,128]{2,0,1:T(8,128)(2,1)}, bf16[64,2,128]{2,0,1:T(8,128)(2,1)S(1)}, u32[]{:S(2)}, u32[]{:S(2)}) collective-permute-start(bf16[64,2,128]{2,0,1:T(8,128)(2,1)} %select_bitcast_fusion.22), channel_id=1, source_target_pairs={{0,4},{4,0},{1,5},{5,1},{2,6},{6,2},{3,7},{7,3},{8,12},{12,8},{9,1... | collective-permute-start | bytes 98312 | tf_op jit(solution)/shard_map/ppermute | solution.py:14
  326.4 11.9 %collective-permute-start.8 = (bf16[64,2,128]{2,0,1:T(8,128)(2,1)}, bf16[64,2,128]{2,0,1:T(8,128)(2,1)S(1)}, u32[]{:S(2)}, u32[]{:S(2)}) collective-permute-start(bf16[64,2,128]{2,0,1:T(8,128)(2,1)} %select_bitcast_fusion.21), channel_id=1, source_target_pairs={{0,8},{8,0},{1,9},{9,1},{2,10},{10,2},{3,11},{11,3},{4,12},{12,4},... | collective-permute-start | bytes 98312 | tf_op jit(solution)/shard_map/ppermute | solution.py:14
  329.6 25.8 %collective-permute-start.9 = (bf16[64,2,128]{2,0,1:T(8,128)(2,1)}, bf16[64,2,128]{2,0,1:T(8,128)(2,1)}, u32[]{:S(2)}, u32[]{:S(2)}) collective-permute-start(bf16[64,2,128]{2,0,1:T(8,128)(2,1)} %select_bitcast_fusion.20), channel_id=1, source_target_pairs={{0,16},{16,0},{1,17},{17,1},{2,18},{18,2},{3,19},{19,3},{4,20},{20... | collective-permute-start | bytes 98312 | tf_op jit(solution)/shard_map/ppermute | solution.py:14
  381.2 4.9 %collective-permute-start.12 = (bf16[64,2,128]{2,0,1:T(8,128)(2,1)S(1)}, bf16[64,2,128]{2,0,1:T(8,128)(2,1)S(1)}, u32[]{:S(2)}, u32[]{:S(2)}) collective-permute-start(bf16[64,2,128]{2,0,1:T(8,128)(2,1)S(1)} %select_bitcast_fusion.17), channel_id=1, source_target_pairs={{0,4},{4,0},{1,5},{5,1},{2,6},{6,2},{3,7},{7,3},{8,12},{12,8},{9,1... | collective-permute-start | bytes 98312 | tf_op jit(solution)/shard_map/ppermute | solution.py:14
  381.9 5.6 %collective-permute-start.13 = (bf16[64,2,128]{2,0,1:T(8,128)(2,1)S(1)}, bf16[64,2,128]{2,0,1:T(8,128)(2,1)S(1)}, u32[]{:S(2)}, u32[]{:S(2)}) collective-permute-start(bf16[64,2,128]{2,0,1:T(8,128)(2,1)S(1)} %select_bitcast_fusion.16), channel_id=1, source_target_pairs={{0,8},{8,0},{1,9},{9,1},{2,10},{10,2},{3,11},{11,3},{4,12},{12,4},... | collective-permute-start | bytes 98312 | tf_op jit(solution)/shard_map/ppermute | solution.py:14
  382.8 14.7 %collective-permute-start.14 = (bf16[64,2,128]{2,0,1:T(8,128)(2,1)}, bf16[64,2,128]{2,0,1:T(8,128)(2,1)}, u32[]{:S(2)}, u32[]{:S(2)}) collective-permute-start(bf16[64,2,128]{2,0,1:T(8,128)(2,1)} %select_bitcast_fusion.15), channel_id=1, source_target_pairs={{0,16},{16,0},{1,17},{17,1},{2,18},{18,2},{3,19},{19,3},{4,20},{20... | collective-permute-start | bytes 98312 | tf_op jit(solution)/shard_map/ppermute | solution.py:14
  (89 other events, 791.1 us)
Sparse Core Ops, SparseCore 0:
  406.2 62.4 all-gather.2
